TPU v7x, 32 devices: a whole 2x2x4 slice. The times are simulated.
32 devices in a mesh: row: 8 (over y, x, core), col: 4 (over z).
Axes of the slice: x: 2, y: 2, z: 4, core: 2. Of those that a mesh axis runs over, the one named last changes fastest.
Arguments:
- matrix: float32 [12288, 12288], P('row', 'col'), may hold values from -10 to 10, as said below
- panel: float32 [12288, 64], P('row'), may hold values from -1.12763724 to 1.12763724
Outputs:
- updated: float32 [12288, 12288], P('row', 'col')
- band_block: float32 [64, 64], replicated
Inputs may be any that keep to these rules, and one draw needn't show every extreme that they name: matrix is exactly symmetric.
All inputs are finite; a program needn't handle non-finite values.
Results may differ from a plain program's by a relative error of at most 0.0002.
Values sent between devices are 32-bit elements; how exact they have to be, the bound alone decides.
No kernel may reach another device: no remote copies, remote signals or barrier semaphores. Data moves between devices by JAX's collectives and lax.ppermute only.
A program may use at most 128 MiB of HBM per device.

v0:
```python
import jax
import jax.numpy as jnp
from jax import lax
from jax.sharding import PartitionSpec as P

precise = lax.Precision.HIGHEST


def upper_cholesky(gram_block):
    order_now = gram_block.shape[0]
    positions = jnp.arange(order_now)

    def one_column(column_index, lower_part):
        gram_column = lax.dynamic_slice_in_dim(gram_block, column_index, 1, 1)[:, 0]
        lower_row = lax.dynamic_slice_in_dim(lower_part, column_index, 1, 0)[0]
        earlier = jnp.where(positions < column_index, lower_row, 0.0)
        reduced = gram_column - jnp.dot(lower_part, earlier, precision=precise)
        pivot_value = jnp.sum(jnp.where(positions == column_index, reduced, 0.0))
        diagonal_value = jnp.sqrt(pivot_value)
        new_column = jnp.where(positions > column_index, reduced / diagonal_value, 0.0) + jnp.where(
            positions == column_index, diagonal_value, 0.0
        )
        return jnp.where(positions[None, :] == column_index, new_column[:, None], lower_part)

    lower_part = lax.fori_loop(
        0, order_now, one_column, jnp.zeros((order_now, order_now), jnp.float32)
    )
    return lower_part.T


def upper_inverse(upper_block):
    order_now = upper_block.shape[0]
    positions = jnp.arange(order_now)

    def one_row(step_count, inverse_part):
        row_at = order_now - 1 - step_count
        upper_row = lax.dynamic_slice_in_dim(upper_block, row_at, 1, 0)[0]
        diagonal_value = jnp.sum(jnp.where(positions == row_at, upper_row, 0.0))
        beyond = jnp.where(positions > row_at, upper_row, 0.0)
        unit_row = jnp.where(positions == row_at, 1.0, 0.0)
        new_row = (unit_row - jnp.dot(beyond, inverse_part, precision=precise)) / diagonal_value
        return jnp.where(positions[:, None] == row_at, new_row[None, :], inverse_part)

    return lax.fori_loop(0, order_now, one_row, jnp.zeros((order_now, order_now), jnp.float32))


def small_factor(block_in):
    order_now = block_in.shape[0]
    positions = jnp.arange(order_now)

    def one_pivot(pivot_index, state_pair):
        working, lower_whole = state_pair
        pivot_column = lax.dynamic_slice_in_dim(working, pivot_index, 1, 1)[:, 0]
        pivot_row = lax.dynamic_slice_in_dim(working, pivot_index, 1, 0)[0]
        pivot_value = jnp.sum(jnp.where(positions == pivot_index, pivot_column, 0.0))
        multipliers = jnp.where(positions > pivot_index, pivot_column / pivot_value, 0.0)
        lower_whole = lower_whole + multipliers[:, None] * (
            positions[None, :] == pivot_index
        ).astype(jnp.float32)
        working = working - multipliers[:, None] * pivot_row[None, :]
        return (working, lower_whole)

    working, lower_whole = lax.fori_loop(
        0, order_now, one_pivot, (block_in, jnp.eye(order_now, dtype=jnp.float32))
    )
    return (lower_whole, jnp.triu(working))


def body(matrix, panel):
    local_rows, local_columns = matrix.shape
    panel_width = panel.shape[1]
    row_index = lax.axis_index("row")
    current_column_index = lax.axis_index("col")
    local_inner = jnp.dot(panel.T, panel, precision=precise)
    head_rows = panel[:panel_width]
    masked = jnp.where(row_index == 0, head_rows, 0.0)
    total_inner, head_rows = lax.psum((local_inner, masked), "row")
    band_factor = -upper_cholesky(total_inner)
    factor_inverse = upper_inverse(band_factor)
    orthogonal_rows = jnp.dot(panel, factor_inverse, precision=precise)
    orthogonal_head = jnp.dot(head_rows, factor_inverse, precision=precise)
    identity = jnp.eye(panel_width, dtype=jnp.float32)
    lower_whole, upper_whole = small_factor(orthogonal_head - identity)
    global_rows = row_index * local_rows + jnp.arange(local_rows)
    unit_rows = (global_rows[:, None] == jnp.arange(panel_width)[None, :]).astype(jnp.float32)
    reflect_rows = jnp.dot(
        orthogonal_rows - unit_rows, upper_inverse(upper_whole), precision=precise
    )
    triangle = -jnp.dot(upper_whole, upper_inverse(lower_whole.T), precision=precise)
    gathered_reflect = lax.all_gather(reflect_rows, "row", axis=0, tiled=True)
    reflect_columns = lax.dynamic_slice_in_dim(
        gathered_reflect, current_column_index * local_columns, local_columns, 0
    )
    partial_product = lax.dot_general(
        matrix, reflect_rows, (((0,), (0,)), ((), ())), precision=precise
    )
    product = lax.psum(partial_product, "row")
    applied_cols = jnp.dot(product, triangle, precision=precise)
    inner_part = jnp.dot(reflect_columns.T, applied_cols, precision=precise)
    inner_total = lax.psum(inner_part, "col")
    coupling = jnp.dot(triangle.T, inner_total, precision=precise)
    corrected_cols = applied_cols - 0.5 * jnp.dot(reflect_columns, coupling, precision=precise)
    gathered_corrected = lax.all_gather(corrected_cols, "col", axis=0, tiled=True)
    corrected_rows = lax.dynamic_slice_in_dim(
        gathered_corrected, row_index * local_rows, local_rows, 0
    )
    left_factor = jnp.concatenate([reflect_rows, corrected_rows], 1)
    right_factor = jnp.concatenate([corrected_cols, reflect_columns], 1)
    updated = matrix - lax.dot_general(
        left_factor, right_factor, (((1,), (1,)), ((), ())), precision=precise
    )
    return (updated, band_factor)


def solution(mesh):
    return jax.shard_map(
        body,
        mesh=mesh,
        in_specs=(P("row", "col"), P("row", None)),
        out_specs=(P("row", "col"), P()),
        check_vma=False,
    )
```

profile of v0, /device:TPU:0, one launch (start us, length us, event | category | flops | bytes accessed | tf_op | source)
XLA Modules:
  0.0 656.6 jit_solution(17921866801268675758)
XLA Ops:
  7.2 1.6 fusion.69
  9.8 26.1 %all-reduce = (f32[64,64]{1,0:T(8,128)S(1)}, f32[64,64]{1,0:T(8,128)S(1)}) all-reduce(f32[64,64]{1,0:T(8,128)S(1)} %fusion.69, f32[64,64]{1,0:T(8,128)S(1)} %broadcast_select_fusion.2), channel_id=1, replica_groups=mesh['row'=8,'col'=4] {'row'}, use_global_device_ids=true, to_apply=%region_0.1 | all-reduce | flops 8192 | bytes 65536 | tf_op jit(solution)/shard_map/psum | solution.py:77
  36.0 102.3 %while.84 = (s32[]{:T(128)}, f32[64,64]{1,0:T(8,128)S(1)}, f32[64,64]{0,1:T(8,128)S(1)}, s32[]{:T(128)}, s32[]{:T(128)}) while((s32[]{:T(128)}, f32[64,64]{1,0:T(8,128)S(1)}, f32[64,64]{0,1:T(8,128)S(1)}, s32[]{:T(128)}, s32[]{:T(128)}) %tuple.192), condition=%wide.region_3.4_spmd.clone.clone, body=%wide.region_1.0_spmd.clone.clone.sunk | while | flops 62274 | bytes 102632 | solution.py:25
  36.1 0.8 select_reduce_fusion.2
  37.7 0.8 select_reduce_fusion.2
  39.2 0.8 select_reduce_fusion.2
  40.8 0.8 select_reduce_fusion.2
  42.4 0.8 select_reduce_fusion.2
  44.0 0.8 select_reduce_fusion.2
  45.6 0.8 select_reduce_fusion.2
  47.2 0.8 select_reduce_fusion.2
  48.8 0.8 select_reduce_fusion.2
  50.4 0.8 select_reduce_fusion.2
  52.0 0.8 select_reduce_fusion.2
  53.6 0.8 select_reduce_fusion.2
  55.2 0.8 select_reduce_fusion.2
  56.8 0.8 select_reduce_fusion.2
  58.4 0.8 select_reduce_fusion.2
  60.0 0.8 select_reduce_fusion.2
  61.6 0.8 select_reduce_fusion.2
  66.4 0.8 select_reduce_fusion.2
  71.2 0.8 select_reduce_fusion.2
  72.8 0.8 select_reduce_fusion.2
  77.6 0.8 select_reduce_fusion.2
  84.0 0.8 select_reduce_fusion.2
  90.4 0.8 select_reduce_fusion.2
  96.8 0.8 select_reduce_fusion.2
  101.6 0.8 select_reduce_fusion.2
  103.2 0.8 select_reduce_fusion.2
  108.0 0.8 select_reduce_fusion.2
  114.4 0.8 select_reduce_fusion.2
  120.7 0.8 select_reduce_fusion.2
  127.1 0.8 select_reduce_fusion.2
  131.9 0.8 select_reduce_fusion.2
  133.5 0.8 select_reduce_fusion.2
  138.4 95.1 %while.85 = (s32[]{:T(128)}, f32[64,64]{1,0:T(8,128)S(1)}, f32[64,64]{1,0:T(8,128)S(1)}, s32[]{:T(128)}, s32[]{:T(128)}, /*index=5*/s32[]{:T(128)}, s32[]{:T(128)}) while((s32[]{:T(128)}, f32[64,64]{1,0:T(8,128)S(1)}, f32[64,64]{1,0:T(8,128)S(1)}, s32[]{:T(128)}, s32[]{:T(128)}, /*index=5*/s32[]{:T(128)}, ...), condition=%wide.region_6.7_spmd.clone.clone, body=%wide.region_4.6_spmd.clone.clone.sunk | while | flops 62086 | bytes 69153 | solution.py:44
  233.7 100.6 %while.83 = (s32[]{:T(128)}, f32[64,64]{0,1:T(8,128)S(1)}, f32[64,64]{0,1:T(8,128)S(1)}, s32[]{:T(128)}) while((s32[]{:T(128)}, f32[64,64]{0,1:T(8,128)S(1)}, f32[64,64]{0,1:T(8,128)S(1)}, s32[]{:T(128)}) %tuple.198), condition=%wide.region_10.11_spmd.clone.clone, body=%wide.region_8.10_spmd.clone.clone.sunk | while | flops 16897 | bytes 69965 | solution.py:63
  334.5 95.1 %while.86 = (s32[]{:T(128)}, f32[64,64]{1,0:T(8,128)S(1)}, f32[64,64]{1,0:T(8,128)S(1)}, s32[]{:T(128)}, s32[]{:T(128)}, /*index=5*/s32[]{:T(128)}, s32[]{:T(128)}) while((s32[]{:T(128)}, f32[64,64]{1,0:T(8,128)S(1)}, f32[64,64]{1,0:T(8,128)S(1)}, s32[]{:T(128)}, s32[]{:T(128)}, /*index=5*/s32[]{:T(128)}, ...), condition=%wide.region_13.14_spmd.clone.clone, body=%wide.region_11.13_spmd.clone.clone.sunk | while | flops 62086 | bytes 69153 | solution.py:44
  429.6 1.5 fusion.59
  431.7 15.5 %convolution_bitcast_fusion.4 = f32[3072,64]{0,1:T(8,128)} fusion(f32[1536,64]{0,1:T(8,128)S(1)} %fusion.70, f32[1536,3072]{1,0:T(8,128)} %param.12), kind=kOutput, calls=%fused_computation.84 | convolution fusion | flops 3623878656 | bytes 20054016 | tf_op jit(solution)/shard_map/dot_general | solution.py:94
  448.0 94.6 %while.87 = (s32[]{:T(128)}, f32[64,64]{1,0:T(8,128)S(1)}, f32[64,64]{1,0:T(8,128)S(1)}, s32[]{:T(128)}, s32[]{:T(128)}, /*index=5*/s32[]{:T(128)}, s32[]{:T(128)}) while((s32[]{:T(128)}, f32[64,64]{1,0:T(8,128)S(1)}, f32[64,64]{1,0:T(8,128)S(1)}, s32[]{:T(128)}, s32[]{:T(128)}, /*index=5*/s32[]{:T(128)}, ...), condition=%wide.region_17.18_spmd.clone.clone, body=%wide.region_15.17_spmd.clone.clone.sunk | while | flops 62086 | bytes 69153 | solution.py:44
  542.8 2.0 fusion.71
  544.8 1.2 constant_dynamic-slice_fusion.8
  546.8 19.3 %psum.31 = f32[64,64]{1,0:T(8,128)S(1)} all-reduce(f32[64,64]{1,0:T(8,128)S(1)} %fusion.72), channel_id=1, replica_groups=mesh['row'=8,'col'=4] {'col'}, use_global_device_ids=true, to_apply=%region_18.19 | all-reduce | flops 4096 | bytes 32768 | tf_op jit(solution)/shard_map/psum | solution.py:100
  566.3 1.7 fusion.58
  568.0 60.0 %all-gather.5.cloned.1.call-done = f32[12288,64]{0,1:T(8,128)} async-done(((f32[3072,64]{0,1:T(8,128)}), f32[12288,64]{0,1:T(8,128)}) %all-gather.5.cloned.1.call-update) | async-done | bytes 3145744 | tf_op jit(solution)/shard_map/all_gather | solution.py:103
  628.0 1.0 constant_dynamic-slice_fusion.7
  629.0 21.1 %convolution_subtract_fusion = f32[1536,3072]{1,0:T(8,128)} fusion(f32[1536,3072]{1,0:T(8,128)} %param.12, f32[3072,64]{0,1:T(8,128)S(1)} %constant_dynamic-slice_fusion.8, f32[3072,64]{0,1:T(8,128)} %fusion.58, f32[1536,64]{0,1:T(8,128)S(1)} %constant_dynamic-slice_fusion.7, f32[1536,64]{0,1:T(8,128)} %copy-done), kind=kOutput, calls=%fused_computation.81 | convolution fusion | flops 7253065728 | bytes 40108032 | tf_op jit(solution)/shard_map/dot_general | solution.py:109
  (1410 shorter events, 417.5 us)
Async XLA Ops:
  7.2 535.6 %all-reduce.3.cloned.1.call-start = ((), (), s32[]{:S(2)}) async-start(), calls=%async_computation | async-start | bytes 1572864 | tf_op jit(solution)/shard_map/psum | solution.py:97
  233.5 416.6 %copy-start.1 = (f32[64,64]{1,0:T(8,128)}, f32[64,64]{1,0:T(8,128)S(1)}, u32[]{:S(2)}) copy-start(f32[64,64]{1,0:T(8,128)S(1)} %get-tuple-element.894) | copy-start | bytes 49156
  431.7 15.6 %copy-start = (f32[1536,64]{0,1:T(8,128)}, f32[1536,64]{0,1:T(8,128)S(1)}, u32[]{:S(2)}) copy-start(f32[1536,64]{0,1:T(8,128)S(1)} %fusion.70) | copy-start | bytes 1179652
  447.2 97.6 %all-gather.3.cloned.1.call-start = ((), (), s32[]{:S(2)}) async-start(), calls=%async_computation.1 | async-start | bytes 3538944 | tf_op jit(solution)/shard_map/all_gather | solution.py:90
  448.0 180.0 %all-gather.5.cloned.1.call-start = ((), (), s32[]{:S(2)}) async-start(), calls=%async_computation.2 | async-start | bytes 3932160 | tf_op jit(solution)/shard_map/all_gather | solution.py:103
Sparse Core Ops, SparseCore 0:
  447.3 55.3 all-reduce.2
  504.6 31.5 all-gather.2
  568.1 59.7 all-gather.4
where the time goes:
time: 660 us; the launch traced here: 657 us
  matrix products  245 us (37%)
  other arithmetic  228 us (35%)
  waiting for transfers between devices  60.7 us (9%)
  loops' own time  48.6 us (7%)
  blocking collectives  45.3 us (7%)
  local copies, waits for them, and re-layouts  14.7 us (2%)
  between operations  14 us (2%)
    dot_general x192, matrix products, one_row(): jnp.dot(beyond, inverse_part, precision=precise)  148 us
    reduce_sum x192, other arithmetic, one_row(): diagonal_value = jnp.sum(jnp.where(positions == row_at, upper_row, 0.0))  120 us
    all_gather x1, waiting for transfers between devices, body(): lax.all_gather(corrected_cols, 'col', axis=0, tiled=True)  60 us
    dot_general x64, matrix products, one_column(): reduced = gram_column - jnp.dot(lower_part, earlier, precision=precise)  51.2 us
    another operation x1, loops' own time, upper_cholesky(): lax.fori_loop(0, order_now, one_column, jnp.zeros((order_now, order_now),...  45 us
    mul x64, other arithmetic, one_pivot(): working = working - multipliers[:, None] * pivot_row[None, :]  41.9 us
    reduce_sum x64, other arithmetic, one_pivot(): jnp.sum(jnp.where(positions == pivot_index, pivot_column, 0.0))  38.8 us
    psum x1, blocking collectives, body(): total_inner, head_rows = lax.psum((local_inner, masked), 'row')  26.1 us
  transfers between devices with their start and end apart: 3, of which 1 were waited for; matrix products, arithmetic and copies ran while one was open for 15% of the time, Pallas kernels for 0%

commit v1 on v0

--- a/solution.py
+++ b/solution.py
@@ -100,7 +100,9 @@
     inner_total = lax.psum(inner_part, "col")
     coupling = jnp.dot(triangle.T, inner_total, precision=precise)
     corrected_cols = applied_cols - 0.5 * jnp.dot(reflect_columns, coupling, precision=precise)
-    gathered_corrected = lax.all_gather(corrected_cols, "col", axis=0, tiled=True)
+    gathered_corrected = jnp.concatenate(
+        lax.all_to_all(jnp.stack([corrected_cols] * lax.axis_size("col")), "col", 0, 0), axis=0
+    )
     corrected_rows = lax.dynamic_slice_in_dim(
         gathered_corrected, row_index * local_rows, local_rows, 0
     )

time: 660 us -> 670 us (1.015)
    all_to_all x0 -> x1, waiting for transfers between devices: none -> 64.5 us  [body(): lax.all_to_all(jnp.stack([corrected_cols] * lax.axis_size('col')), 'col',...]
    all_gather x1 -> x0, waiting for transfers between devices: 60 us -> none  [body(): lax.all_gather(corrected_cols, 'col', axis=0, tiled=True)]
  transfers between devices with their start and end apart: 3 -> 3, of which waited for: 1 -> 1; matrix products, arithmetic and copies ran while one was open for 15% -> 14% of each run, Pallas kernels for 0% -> 0%
where the time goes in v1:
time: 670 us; the launch traced here: 667 us
  matrix products  242 us (36%)
  other arithmetic  228 us (34%)
  waiting for transfers between devices  65.2 us (10%)
  loops' own time  48.6 us (7%)
  blocking collectives  45.3 us (7%)
  local copies, waits for them, and re-layouts  18.7 us (3%)
  between operations  14.3 us (2%)
    dot_general x192, matrix products, one_row(): jnp.dot(beyond, inverse_part, precision=precise)  148 us
    reduce_sum x192, other arithmetic, one_row(): diagonal_value = jnp.sum(jnp.where(positions == row_at, upper_row, 0.0))  120 us
    all_to_all x1, waiting for transfers between devices, body(): lax.all_to_all(jnp.stack([corrected_cols] * lax.axis_size('col')), 'col',...  64.5 us
    dot_general x64, matrix products, one_column(): reduced = gram_column - jnp.dot(lower_part, earlier, precision=precise)  51.2 us
    another operation x1, loops' own time, upper_cholesky(): lax.fori_loop(0, order_now, one_column, jnp.zeros((order_now, order_now),...  45 us
    mul x64, other arithmetic, one_pivot(): working = working - multipliers[:, None] * pivot_row[None, :]  41.9 us
    reduce_sum x64, other arithmetic, one_pivot(): jnp.sum(jnp.where(positions == pivot_index, pivot_column, 0.0))  38.8 us
    psum x1, blocking collectives, body(): total_inner, head_rows = lax.psum((local_inner, masked), 'row')  26.1 us
  transfers between devices with their start and end apart: 3, of which 1 were waited for; matrix products, arithmetic and copies ran while one was open for 14% of the time, Pallas kernels for 0%

profile of v1, /device:TPU:0, one launch (start us, length us, event | category | flops | bytes accessed | tf_op | source)
XLA Modules:
  0.0 666.7 jit_solution(12224079568297718163)
XLA Ops:
  7.2 1.7 fusion.69
  9.8 26.1 %all-reduce = (f32[64,64]{1,0:T(8,128)S(1)}, f32[64,64]{1,0:T(8,128)S(1)}) all-reduce(f32[64,64]{1,0:T(8,128)S(1)} %fusion.69, f32[64,64]{1,0:T(8,128)S(1)} %broadcast_select_fusion.2), channel_id=1, replica_groups=mesh['row'=8,'col'=4] {'row'}, use_global_device_ids=true, to_apply=%region_0.1 | all-reduce | flops 8192 | bytes 65536 | tf_op jit(solution)/shard_map/psum | solution.py:77
  36.0 102.2 %while.84 = (s32[]{:T(128)}, f32[64,64]{1,0:T(8,128)S(1)}, f32[64,64]{0,1:T(8,128)S(1)}, s32[]{:T(128)}, s32[]{:T(128)}) while((s32[]{:T(128)}, f32[64,64]{1,0:T(8,128)S(1)}, f32[64,64]{0,1:T(8,128)S(1)}, s32[]{:T(128)}, s32[]{:T(128)}) %tuple.194), condition=%wide.region_3.4_spmd.clone.clone, body=%wide.region_1.0_spmd.clone.clone.sunk | while | flops 62274 | bytes 102632 | solution.py:25
  36.1 0.8 select_reduce_fusion.2
  37.7 0.8 select_reduce_fusion.2
  39.3 0.8 select_reduce_fusion.2
  40.9 0.8 select_reduce_fusion.2
  42.5 0.8 select_reduce_fusion.2
  44.1 0.8 select_reduce_fusion.2
  45.7 0.8 select_reduce_fusion.2
  47.3 0.8 select_reduce_fusion.2
  48.9 0.8 select_reduce_fusion.2
  50.5 0.8 select_reduce_fusion.2
  52.1 0.8 select_reduce_fusion.2
  53.7 0.8 select_reduce_fusion.2
  55.2 0.8 select_reduce_fusion.2
  56.8 0.8 select_reduce_fusion.2
  61.6 0.8 select_reduce_fusion.2
  64.8 0.8 select_reduce_fusion.2
  72.8 0.8 select_reduce_fusion.2
  76.0 0.8 select_reduce_fusion.2
  84.0 0.8 select_reduce_fusion.2
  87.2 0.8 select_reduce_fusion.2
  92.0 0.8 select_reduce_fusion.2
  95.2 0.8 select_reduce_fusion.2
  103.2 0.8 select_reduce_fusion.2
  106.4 0.8 select_reduce_fusion.2
  114.4 0.8 select_reduce_fusion.2
  117.5 0.8 select_reduce_fusion.2
  122.3 0.8 select_reduce_fusion.2
  125.5 0.8 select_reduce_fusion.2
  133.5 0.8 select_reduce_fusion.2
  136.7 0.8 select_reduce_fusion.2
  138.4 95.1 %while.85 = (s32[]{:T(128)}, f32[64,64]{1,0:T(8,128)S(1)}, f32[64,64]{1,0:T(8,128)S(1)}, s32[]{:T(128)}, s32[]{:T(128)}, /*index=5*/s32[]{:T(128)}, s32[]{:T(128)}) while((s32[]{:T(128)}, f32[64,64]{1,0:T(8,128)S(1)}, f32[64,64]{1,0:T(8,128)S(1)}, s32[]{:T(128)}, s32[]{:T(128)}, /*index=5*/s32[]{:T(128)}, ...), condition=%wide.region_6.7_spmd.clone.clone, body=%wide.region_4.6_spmd.clone.clone.sunk | while | flops 62086 | bytes 69153 | solution.py:44
  234.3 100.6 %while.83 = (s32[]{:T(128)}, f32[64,64]{0,1:T(8,128)S(1)}, f32[64,64]{0,1:T(8,128)S(1)}, s32[]{:T(128)}) while((s32[]{:T(128)}, f32[64,64]{0,1:T(8,128)S(1)}, f32[64,64]{0,1:T(8,128)S(1)}, s32[]{:T(128)}) %tuple.200), condition=%wide.region_10.11_spmd.clone.clone, body=%wide.region_8.10_spmd.clone.clone.sunk | while | flops 16897 | bytes 69965 | solution.py:63
  335.1 95.1 %while.86 = (s32[]{:T(128)}, f32[64,64]{1,0:T(8,128)S(1)}, f32[64,64]{1,0:T(8,128)S(1)}, s32[]{:T(128)}, s32[]{:T(128)}, /*index=5*/s32[]{:T(128)}, s32[]{:T(128)}) while((s32[]{:T(128)}, f32[64,64]{1,0:T(8,128)S(1)}, f32[64,64]{1,0:T(8,128)S(1)}, s32[]{:T(128)}, s32[]{:T(128)}, /*index=5*/s32[]{:T(128)}, ...), condition=%wide.region_13.14_spmd.clone.clone, body=%wide.region_11.13_spmd.clone.clone.sunk | while | flops 62086 | bytes 69153 | solution.py:44
  431.3 15.5 %convolution_bitcast_fusion.4 = f32[3072,64]{0,1:T(8,128)} fusion(f32[1536,64]{0,1:T(8,128)S(1)} %fusion.70, f32[1536,3072]{1,0:T(8,128)} %param.12), kind=kOutput, calls=%fused_computation.84 | convolution fusion | flops 3623878656 | bytes 20054016 | tf_op jit(solution)/shard_map/dot_general | solution.py:94
  447.6 94.6 %while.87 = (s32[]{:T(128)}, f32[64,64]{1,0:T(8,128)S(1)}, f32[64,64]{1,0:T(8,128)S(1)}, s32[]{:T(128)}, s32[]{:T(128)}, /*index=5*/s32[]{:T(128)}, s32[]{:T(128)}) while((s32[]{:T(128)}, f32[64,64]{1,0:T(8,128)S(1)}, f32[64,64]{1,0:T(8,128)S(1)}, s32[]{:T(128)}, s32[]{:T(128)}, /*index=5*/s32[]{:T(128)}, ...), condition=%wide.region_17.18_spmd.clone.clone, body=%wide.region_15.17_spmd.clone.clone.sunk | while | flops 62086 | bytes 69153 | solution.py:44
  542.4 2.0 fusion.71
  544.4 1.2 constant_dynamic-slice_fusion.8
  546.3 19.2 %psum.31 = f32[64,64]{1,0:T(8,128)S(1)} all-reduce(f32[64,64]{1,0:T(8,128)S(1)} %fusion.72), channel_id=1, replica_groups=mesh['row'=8,'col'=4] {'col'}, use_global_device_ids=true, to_apply=%region_18.19 | all-reduce | flops 4096 | bytes 32768 | tf_op jit(solution)/shard_map/psum | solution.py:100
  565.8 0.8 fusion.58
  566.7 0.9 copy-done.2
  567.6 2.0 stack.2
  569.6 3.9 all-to-all-start
  573.5 64.5 %all-to-all-done = f32[4,3072,64]{1,2,0:T(8,128)S(1)} async-done(((f32[4,3072,64]{1,2,0:T(8,128)}), f32[4,3072,64]{1,2,0:T(8,128)S(1)}, u32[]{:S(2)}, u32[]{:S(2)}) %all-to-all-start) | async-done | bytes 3145760 | tf_op jit(solution)/shard_map/all_to_all | solution.py:104
  638.2 0.9 copy-done.1
  639.5 20.4 %convolution_subtract_fusion = f32[1536,3072]{1,0:T(8,128)} fusion(f32[1536,3072]{1,0:T(8,128)} %param.12, f32[3072,64]{0,1:T(8,128)S(1)} %copy-done.1, f32[3072,64]{0,1:T(8,128)S(1)} %copy-done.3, f32[1536,64]{0,1:T(8,128)S(1)} %constant_dynamic-slice_fusion.7, f32[1536,64]{0,1:T(8,128)S(1)} %copy-done.5), kind=kOutput, calls=%fused_computation.81 | convolution fusion | flops 7253065728 | bytes 40108032 | tf_op jit(solution)/shard_map/dot_general | solution.py:111
  (1423 shorter events, 420.8 us)
Async XLA Ops:
  7.2 423.0 %copy-start.6 = (f32[1536,64]{0,1:T(8,128)S(1)}, f32[1536,64]{0,1:T(8,128)}, u32[]{:S(2)}) copy-start(f32[1536,64]{0,1:T(8,128)} %param.13) | copy-start | bytes 1179652
  7.2 535.2 %all-reduce.3.cloned.1.call-start = ((), (), s32[]{:S(2)}) async-start(), calls=%async_computation.1 | async-start | bytes 1572864 | tf_op jit(solution)/shard_map/psum | solution.py:97
  233.5 0.6 copy-start.7
  431.3 15.5 %copy-start.4 = (f32[1536,64]{0,1:T(8,128)}, f32[1536,64]{0,1:T(8,128)S(1)}, u32[]{:S(2)}) copy-start(f32[1536,64]{0,1:T(8,128)S(1)} %fusion.70) | copy-start | bytes 1179652
  446.8 97.5 %all-gather.2.cloned.1.call-start = ((), (), s32[]{:S(2)}) async-start(), calls=%async_computation.2 | async-start | bytes 3538944 | tf_op jit(solution)/shard_map/all_gather | solution.py:90
  545.5 24.1 %copy-start = (f32[3072,64]{0,1:T(8,128)}, f32[3072,64]{0,1:T(8,128)S(1)}, u32[]{:S(2)}) copy-start(f32[3072,64]{0,1:T(8,128)S(1)} %constant_dynamic-slice_fusion.8) | copy-start | bytes 2359300
  566.7 0.9 copy-start.2
  569.6 68.4 %all-to-all-start = ((f32[4,3072,64]{1,2,0:T(8,128)}), f32[4,3072,64]{1,2,0:T(8,128)S(1)}, u32[]{:S(2)}, u32[]{:S(2)}) async-start(f32[4,3072,64]{1,2,0:T(8,128)} %stack.2), calls=%async_computation | async-start | bytes 6291456 | tf_op jit(solution)/shard_map/all_to_all | solution.py:104
  638.0 1.1 copy-start.1
  638.0 1.4 copy-start.3
  638.0 1.5 copy-start.5
Sparse Core Ops, SparseCore 0:
  446.9 55.2 all-reduce.2
  504.2 31.5 all-gather.1
